TPU v7x, 32 devices: a whole 2x2x4 slice. The times are simulated.
32 devices in a mesh: lat: 8 (over y, x, core), lev: 4 (over z).
Axes of the slice: x: 2, y: 2, z: 4, core: 2. Of those that a mesh axis runs over, the one named last changes fastest.
Arguments:
- grid_adjoint: float32 [2, 96, 640, 1280], P(None, 'lev', 'lat'), may hold values from -6 to 6
- trajectory: bfloat16 [2, 96, 640, 1280], P(None, 'lev', 'lat'), may hold values from -5 to 5
- pair_order: int32 [320], replicated, may hold values from 0 to 319, each once
- legendre: bfloat16 [320, 640, 641], P('lat'), may hold values from -0.25 to 0.25
- modes: bfloat16 [96, 96], replicated, may hold values from -0.625 to 0.625
- rates: float32 [96], replicated, may hold values from 0.5 to 50
Outputs:
- grid_out: float32 [2, 96, 640, 1280], P(None, 'lev', 'lat')
Inputs may be any that keep to these rules, and one draw needn't show every extreme that they name: `pair_order`: A permutation: entry s names the pair k and 639 - k whose basis values are row s of legendre.
All inputs are finite; a program needn't handle non-finite values.
Results may differ from a plain program's by a relative error of at most 0.0068.
Values may be sent and summed in bfloat16 or wider, within the bound.
A program may use at most 192 MiB of HBM per device.

v0:
```python
import math
import jax
import jax.numpy as jnp
from jax import lax
from jax.sharding import PartitionSpec as P


def tables(length, number):
    row = lax.broadcasted_iota(jnp.int32, (length, 2 * number), 0)
    col = lax.broadcasted_iota(jnp.int32, (length, 2 * number), 1)
    wavenum = col % number
    phases = 2.0 * math.pi / length * (row * wavenum % length).astype(jnp.float32)
    forward = (jnp.where(col < number, jnp.cos(phases), -jnp.sin(phases)) / length).astype(
        jnp.bfloat16
    )
    inrow = lax.broadcasted_iota(jnp.int32, (2 * number, length), 0)
    position = lax.broadcasted_iota(jnp.int32, (2 * number, length), 1)
    inwave = inrow % number
    inphase = 2.0 * math.pi / length * (position * inwave % length).astype(jnp.float32)
    weights = jnp.where(inwave == 0, 1.0, 2.0).astype(jnp.float32)
    inverse = jnp.where(
        inrow < number, weights * jnp.cos(inphase), -weights * jnp.sin(inphase)
    ).astype(jnp.bfloat16)
    return (forward, inverse)


def degrees(waves_a, truncation):
    column = lax.broadcasted_iota(jnp.int32, (waves_a.shape[0], truncation + 1), 1)
    lower_part = column < (truncation - waves_a)[:, None]
    degree = jnp.where(lower_part, waves_a[:, None] + column, column - 1)
    degree_ratio = (degree * (degree + 1)).astype(jnp.float32) / float(
        truncation * (truncation + 1)
    )
    return (lower_part, degree_ratio)


def per_device(grid_adjoint, trajectory, pair_order, legendre, modes, rates):
    fields, levels, lat_rows, longitudes = grid_adjoint.shape
    wave_count = longitudes // 2
    slot_count = legendre.shape[0]
    lat_count = legendre.shape[1]
    primary = trajectory[0].astype(jnp.float32)
    coupling = trajectory[1].astype(jnp.float32)
    coupled = jnp.stack(
        [
            primary * grid_adjoint[0] + coupling * grid_adjoint[1],
            coupling * grid_adjoint[0] + primary * grid_adjoint[1],
        ]
    ).astype(jnp.bfloat16)
    forward, inverse = tables(longitudes, wave_count)
    fourier_local = jnp.dot(
        coupled.reshape(-1, longitudes), forward, preferred_element_type=jnp.float32
    )
    fourier_local = fourier_local.astype(jnp.bfloat16).reshape(
        fields, levels, lat_rows, 2, wave_count
    )
    column_order = jnp.stack([pair_order, wave_count - 1 - pair_order], axis=1).reshape(-1)
    permuted = jnp.take(fourier_local, column_order, axis=4)
    received_bands = lax.all_to_all(permuted, "lat", split_axis=4, concat_axis=2, tiled=True)
    grouped = received_bands.reshape(fields, levels, lat_count, 2, slot_count, 2)
    band_index = lax.axis_index("lat")
    local_waves = lax.dynamic_slice_in_dim(pair_order, band_index * slot_count, slot_count)
    lower_part, degree_ratio = degrees(local_waves, wave_count)
    products = jnp.einsum(
        "slj,fvlcsh->sfvchj", legendre, grouped, preferred_element_type=jnp.float32
    )
    lower_mask = lower_part[:, None, None, None, :]
    spectral = jnp.where(lower_mask, products[:, :, :, :, 0], products[:, :, :, :, 1])
    damped = spectral[:, 0] / (1.0 + 4.0 * degree_ratio * degree_ratio)[:, None, None, :]
    rounded = spectral[:, 1].astype(jnp.bfloat16)
    level_index = lax.axis_index("lev")
    lev_count = lax.axis_size("lev")
    flattened = jnp.transpose(rounded, (1, 0, 2, 3)).reshape(levels, -1)
    column_total = flattened.shape[1]
    column_width = -(-column_total // lev_count)
    padding = column_width * lev_count - column_total
    padded = jnp.pad(flattened, ((0, 0), (0, padding)))
    columns = lax.all_to_all(padded, "lev", split_axis=1, concat_axis=0, tiled=True)
    ratio_flat = jnp.broadcast_to(
        degree_ratio[:, None, :], (slot_count, 2, wave_count + 1)
    ).reshape(-1)
    ratio_flat = jnp.pad(ratio_flat, (0, padding))
    ratio_piece = lax.dynamic_slice_in_dim(ratio_flat, level_index * column_width, column_width)
    projected = jnp.einsum("km,kn->mn", modes, columns, preferred_element_type=jnp.float32)
    factor = 1.0 / (1.0 + rates[:, None] * ratio_piece[None, :])
    weighted = (projected * factor).astype(jnp.bfloat16)
    solved_columns = jnp.dot(modes, weighted, preferred_element_type=jnp.float32)
    returned_levels = lax.all_to_all(
        solved_columns.astype(jnp.bfloat16), "lev", split_axis=0, concat_axis=1, tiled=True
    ).astype(solved_columns.dtype)
    solved = returned_levels[:, :column_total].reshape(levels, slot_count, 2, wave_count + 1)
    solved = jnp.transpose(solved, (1, 0, 2, 3))
    updated = jnp.stack([damped, solved], axis=1).astype(jnp.bfloat16)
    zero_value = jnp.zeros((), jnp.bfloat16)
    halves = jnp.stack(
        [jnp.where(lower_mask, updated, zero_value), jnp.where(lower_mask, zero_value, updated)],
        axis=-2,
    )
    synthesised = jnp.einsum(
        "slj,sfvchj->fvlcsh", legendre, halves, preferred_element_type=jnp.float32
    )
    synthesised = synthesised.astype(jnp.bfloat16).reshape(
        fields, levels, lat_count, 2, slot_count * 2
    )
    returned = lax.all_to_all(synthesised, "lat", split_axis=2, concat_axis=4, tiled=True)
    inverse_order = (
        jnp.zeros((wave_count,), jnp.int32)
        .at[column_order]
        .set(jnp.arange(wave_count, dtype=jnp.int32))
    )
    natural = jnp.take(returned, inverse_order, axis=4)
    grid_out = jnp.dot(
        natural.reshape(-1, 2 * wave_count), inverse, preferred_element_type=jnp.float32
    )
    return grid_out.reshape(fields, levels, lat_rows, longitudes)


def solution(mesh):
    placed = (
        P(None, "lev", "lat", None),
        P(None, "lev", "lat", None),
        P(),
        P("lat", None, None),
        P(),
        P(),
    )
    return jax.shard_map(
        per_device,
        mesh=mesh,
        in_specs=placed,
        out_specs=P(None, "lev", "lat", None),
        check_vma=False,
    )
```

profile of v0, /device:TPU:0, one launch (start us, length us, event | category | flops | bytes accessed | tf_op | source)
XLA Modules:
  0.0 961.1 jit_solution(389869084658848675)
XLA Ops:
  1.8 14.9 %fusion.9 = (bf16[1,24,80,1280]{3,2,1,0:T(8,128)(2,1)}, bf16[1,24,80,1280]{3,2,1,0:T(8,128)(2,1)}) fusion(f32[2,24,80,1280]{3,2,1,0:T(8,128)} %param.8, bf16[2,24,80,1280]{3,2,1,0:T(8,128)(2,1)} %param.9), kind=kLoop, calls=%fused_computation.25 | loop fusion | flops 24576000 | bytes 39321600 | tf_op jit(solution)/shard_map/convert.8
  25.3 27.6 %multiply_convert_fusion.4 = bf16[1280,1280]{1,0:T(8,128)(2,1)S(1)} fusion(s32[1280]{0:T(1024)S(1)} %get-tuple-element.14, s32[1280]{0:T(1024)S(1)} %get-tuple-element.15, pred[1280]{0:T(1024)(128)(4,1)S(1)} %get-tuple-element.17, pred[1280]{0:T(1024)(128)(4,1)S(1)} %get-tuple-element.16), kind=kLoop, calls=%fused_computation.47.clone.clone.1 | loop fusion | flops 22937600 | bytes 3289600 | tf_op jit(solution)/shard_map/dot_general | solution.py:51
  52.9 19.0 %convolution_convert_fusion.1 = bf16[3840,1280]{1,0:T(8,128)(2,1)} fusion(bf16[3840,1280]{1,0:T(8,128)(2,1)} %bitcast.82, bf16[1280,1280]{1,0:T(8,128)(2,1)S(1)} %multiply_convert_fusion.4), kind=kOutput, calls=%fused_computation.14 | convolution fusion | flops 12587827200 | bytes 22937600 | tf_op jit(solution)/shard_map/dot_general | solution.py:51
  71.9 19.3 %reshape.233 = bf16[2,24,80,2,640]{4,3,2,1,0:T(2,128)(2,1)} reshape(bf16[3840,1280]{1,0:T(8,128)(2,1)} %convolution_convert_fusion.1) | data formatting | bytes 19660800 | tf_op jit(solution)/shard_map/reshape | solution.py:54
  91.2 25.9 %copy.64 = bf16[2,24,80,2,640]{2,1,3,0,4:T(8,128)(2,1)} copy(bf16[2,24,80,2,640]{4,3,2,1,0:T(2,128)(2,1)} %reshape.233) | data formatting | bytes 19660800 | tf_op jit(solution)/shard_map/reshape | solution.py:54
  117.1 25.2 %gather_fusion = bf16[640,2,24,80,2]{3,2,4,1,0:T(8,128)(2,1)} fusion(bf16[2,24,80,2,640]{2,1,3,0,4:T(8,128)(2,1)} %copy.64, s32[1024]{0:T(1024)S(1)} %pad_clamp_fusion.1), kind=kCustom, calls=%fused_computation.clone | custom fusion | bytes 19663360 | tf_op jit(solution)/shard_map/jit(_take)/gather | solution.py:58
  142.3 14.0 %select_bitcast_fusion.1 = bf16[2,24,80,2,640]{2,1,3,0,4:T(8,128)(2,1)} fusion(bf16[640,2,24,80,2]{3,2,4,1,0:T(8,128)(2,1)} %gather_fusion, pred[640]{0:T(1024)(128)(4,1)S(1)} %compare_and_fusion.1), kind=kLoop, calls=%fused_computation.9 | loop fusion | flops 4915200 | bytes 19661440 | tf_op jit(solution)/shard_map/jit(_take)/select_n | solution.py:58
  162.8 172.5 %all-to-all-done = bf16[2,24,80,2,640]{2,1,3,0,4:T(8,128)(2,1)} async-done(((bf16[2,24,80,2,640]{2,1,3,0,4:T(8,128)(2,1)}), bf16[2,24,80,2,640]{2,1,3,0,4:T(8,128)(2,1)}, u32[]{:S(2)}, u32[]{:S(2)}) %all-to-all-start) | async-done | bytes 9830432 | tf_op jit(solution)/shard_map/all_to_all | solution.py:59
  335.4 27.2 %copy.104 = bf16[2,24,80,2,8,80]{2,4,1,5,3,0:T(8,128)(2,1)} copy(bf16[2,24,80,2,8,80]{2,1,3,0,5,4:T(8,128)(2,1)} %bitcast.2) | data formatting | bytes 19660800 | tf_op jit(solution)/shard_map/all_to_all | solution.py:59
  362.6 23.1 %reshape.235 = bf16[2,24,640,2,40,2]{2,1,5,4,3,0:T(8,128)(2,1)} reshape(bf16[2,24,8,80,2,80]{3,2,1,5,4,0:T(8,128)(2,1)} %bitcast.76) | data formatting | bytes 19660800 | tf_op jit(solution)/shard_map/reshape | solution.py:60
  385.6 29.7 %fusion.2 = f32[40,2,24,2,2,641]{5,2,4,3,1,0:T(8,128)} fusion(bf16[40,640,641,1,1,1]{1,0,2,5,4,3:T(8,128)(2,1)} %bitcast.79, bf16[2,24,640,2,40,2]{2,1,5,4,3,0:T(8,128)(2,1)} %reshape.235), kind=kOutput, calls=%fused_computation.5 | convolution fusion | flops 6301286400 | bytes 62341120 | tf_op jit(solution)/shard_map/slj,fvlcsh->sfvchj/dot_general | solution.py:64
  438.8 15.4 %all-to-all-start.1 = ((bf16[24,4,12820]{2,0,1:T(8,128)(2,1)}), bf16[24,4,12820]{2,0,1:T(8,128)(2,1)S(1)}, u32[]{:S(2)}, u32[]{:S(2)}) async-start(bf16[24,4,12820]{2,0,1:T(8,128)(2,1)} %copy.70), calls=%async_computation.1 | async-start | bytes 4964352 | tf_op jit(solution)/shard_map/all_to_all | solution.py:78
  454.8 52.9 %all-to-all-done.1 = bf16[24,4,12820]{2,0,1:T(8,128)(2,1)S(1)} async-done(((bf16[24,4,12820]{2,0,1:T(8,128)(2,1)}), bf16[24,4,12820]{2,0,1:T(8,128)(2,1)S(1)}, u32[]{:S(2)}, u32[]{:S(2)}) %all-to-all-start.1) | async-done | bytes 2461472 | tf_op jit(solution)/shard_map/all_to_all | solution.py:78
  518.7 52.7 %all-to-all-done.2 = bf16[4,24,12820]{2,1,0:T(8,128)(2,1)} async-done(((bf16[4,24,12820]{2,1,0:T(8,128)(2,1)}), bf16[4,24,12820]{2,1,0:T(8,128)(2,1)}, u32[]{:S(2)}, u32[]{:S(2)}) %all-to-all-start.2) | async-done | bytes 2461472 | tf_op jit(solution)/shard_map/all_to_all | solution.py:88
  591.3 22.3 %convert_bitcast_fusion = bf16[2,24,640,2,40,2]{2,1,5,3,0,4:T(8,128)(2,1)} fusion(bf16[40,640,641,1,1,1]{1,0,2,5,4,3:T(8,128)(2,1)} %bitcast.80, bf16[40,2,24,2,1,641]{5,2,3,0,4,1:T(8,128)(2,1)S(1)} %get-tuple-element.11, bf16[40,2,24,2,1,641]{5,2,3,0,4,1:T(8,128)(2,1)S(1)} %get-tuple-element.10), kind=kOutput, calls=%fused_computation.31 | convolution fusion | flops 6311124480 | bytes 52495360 | tf_op jit(solution)/shard_map/slj,sfvchj->fvlcsh/dot_general | solution.py:99
  622.0 20.1 %copy.76 = bf16[2,24,640,2,80]{4,1,3,0,2:T(8,128)(2,1)} copy(bf16[2,24,640,2,80]{2,1,4,3,0:T(8,128)(2,1)} %bitcast.78) | data formatting | bytes 19660800 | tf_op jit(solution)/shard_map/reshape | solution.py:102
  652.5 30.0 %fusion.83 = bf16[1280,1280,1,1]{1,0,3,2:T(8,128)(2,1)S(1)} fusion(s32[1280]{0:T(1024)S(1)} %copy-done.6, s32[1280]{0:T(1024)S(1)} %copy-done.8, pred[1280]{0:T(1024)(128)(4,1)S(1)} %copy-done.12, pred[1280]{0:T(1024)(128)(4,1)S(1)} %copy-done.10), kind=kLoop, calls=%fused_computation.59.clone.clone.1 | loop fusion | flops 27852800 | bytes 3289600 | tf_op jit(solution)/shard_map/dot_general | solution.py:112
  682.5 138.4 %all-to-all-done.3 = bf16[2,24,640,2,80]{4,1,3,0,2:T(8,128)(2,1)} async-done(((bf16[2,24,640,2,80]{4,1,3,0,2:T(8,128)(2,1)}), bf16[2,24,640,2,80]{4,1,3,0,2:T(8,128)(2,1)}, u32[]{:S(2)}, u32[]{:S(2)}) %all-to-all-start.3) | async-done | bytes 9830432 | tf_op jit(solution)/shard_map/all_to_all | solution.py:105
  820.9 33.7 %copy.87 = bf16[2,24,80,2,8,80]{2,1,3,0,5,4:T(8,128)(2,1)} copy(bf16[2,24,80,2,8,80]{5,1,3,0,2,4:T(8,128)(2,1)} %bitcast.31) | data formatting | bytes 19660800 | tf_op jit(solution)/shard_map/all_to_all | solution.py:105
  854.6 25.0 %gather_fusion.1 = bf16[640,2,24,80,2]{3,2,4,1,0:T(8,128)(2,1)} fusion(bf16[2,24,80,2,640]{2,1,3,0,4:T(8,128)(2,1)} %bitcast.77, s32[1024]{0:T(1024)S(1)} %pad_clamp_fusion), kind=kCustom, calls=%fused_computation.1.clone | custom fusion | bytes 19663360 | tf_op jit(solution)/shard_map/jit(_take)/gather | solution.py:111
  879.5 14.0 %select_bitcast_fusion = bf16[2,24,80,2,640]{2,1,3,0,4:T(8,128)(2,1)} fusion(bf16[640,2,24,80,2]{3,2,4,1,0:T(8,128)(2,1)} %gather_fusion.1, pred[640]{0:T(1024)(128)(4,1)S(1)} %compare_and_fusion), kind=kLoop, calls=%fused_computation.8 | loop fusion | flops 4915200 | bytes 19661440 | tf_op jit(solution)/shard_map/jit(_take)/select_n | solution.py:111
  893.6 26.9 %copy.79 = bf16[2,24,80,2,640]{4,3,2,1,0:T(2,128)(2,1)} copy(bf16[2,24,80,2,640]{2,1,3,0,4:T(8,128)(2,1)} %select_bitcast_fusion) | data formatting | bytes 19660800 | tf_op jit(solution)/shard_map/jit(_take)/select_n | solution.py:111
  920.5 21.8 %dot_general.28 = bf16[2,24,80,1280]{3,2,1,0:T(8,128)(2,1)} reshape(bf16[2,24,80,2,640]{4,3,2,1,0:T(2,128)(2,1)} %copy.79) | data formatting | bytes 19660800 | tf_op jit(solution)/shard_map/dot_general | solution.py:112
  942.3 18.3 %fusion.33 = f32[2,24,80,1280]{3,2,1,0:T(8,128)} fusion(bf16[2,24,80,1280]{3,2,1,0:T(8,128)(2,1)} %dot_general.28, bf16[1280,1280,1,1]{1,0,3,2:T(8,128)(2,1)S(1)} %fusion.83), kind=kOutput, calls=%fused_computation.60 | convolution fusion | flops 12582912000 | bytes 32768000 | tf_op jit(solution)/shard_map/dot_general | solution.py:112
  (69 shorter events, 90.5 us)
Async XLA Ops:
  0.0 507.7 %copy-start = (bf16[96,96]{1,0:T(8,128)(2,1)S(1)}, bf16[96,96]{1,0:T(8,128)(2,1)}, u32[]{:S(2)}) copy-start(bf16[96,96]{1,0:T(8,128)(2,1)} %param.12) | copy-start | bytes 55300
  0.0 25.3 %copy-start.5 = (s32[1280]{0:T(1024)}, s32[1280]{0:T(1024)S(1)}, u32[]{:S(2)}) copy-start(s32[1280]{0:T(1024)S(1)} %get-tuple-element.14) | copy-start | bytes 15364
  0.0 25.3 %copy-start.7 = (s32[1280]{0:T(1024)}, s32[1280]{0:T(1024)S(1)}, u32[]{:S(2)}) copy-start(s32[1280]{0:T(1024)S(1)} %get-tuple-element.15) | copy-start | bytes 15364
  0.0 25.2 %copy-start.9 = (pred[1280]{0:T(1024)(128)(4,1)}, pred[1280]{0:T(1024)(128)(4,1)S(1)}, u32[]{:S(2)}) copy-start(pred[1280]{0:T(1024)(128)(4,1)S(1)} %get-tuple-element.16) | copy-start | bytes 3844
  0.1 25.2 %copy-start.11 = (pred[1280]{0:T(1024)(128)(4,1)}, pred[1280]{0:T(1024)(128)(4,1)S(1)}, u32[]{:S(2)}) copy-start(pred[1280]{0:T(1024)(128)(4,1)S(1)} %get-tuple-element.17) | copy-start | bytes 3844
  1.6 15.0 %copy-start.3 = (s32[320,2]{1,0:T(8,128)}, s32[320,2]{1,0:T(8,128)S(1)}, u32[]{:S(2)}) copy-start(s32[320,2]{1,0:T(8,128)S(1)} %copy.62) | copy-start | bytes 7684
  156.3 179.0 %all-to-all-start = ((bf16[2,24,80,2,640]{2,1,3,0,4:T(8,128)(2,1)}), bf16[2,24,80,2,640]{2,1,3,0,4:T(8,128)(2,1)}, u32[]{:S(2)}, u32[]{:S(2)}) async-start(bf16[2,24,80,2,640]{2,1,3,0,4:T(8,128)(2,1)} %select_bitcast_fusion.1), calls=%async_computation | async-start | bytes 31457280 | tf_op jit(solution)/shard_map/all_to_all | solution.py:59
  424.5 4.5 copy-start.2
  435.4 72.3 %copy-start.13 = (f32[96]{0:T(128)S(1)}, f32[96]{0:T(128)}, u32[]{:S(2)}) copy-start(f32[96]{0:T(128)} %param.13) | copy-start | bytes 1156
  438.8 68.9 %all-to-all-start.1 = ((bf16[24,4,12820]{2,0,1:T(8,128)(2,1)}), bf16[24,4,12820]{2,0,1:T(8,128)(2,1)S(1)}, u32[]{:S(2)}, u32[]{:S(2)}) async-start(bf16[24,4,12820]{2,0,1:T(8,128)(2,1)} %copy.70), calls=%async_computation.1 | async-start | bytes 4964352 | tf_op jit(solution)/shard_map/all_to_all | solution.py:78
  510.7 60.6 %all-to-all-start.2 = ((bf16[4,24,12820]{2,1,0:T(8,128)(2,1)}), bf16[4,24,12820]{2,1,0:T(8,128)(2,1)}, u32[]{:S(2)}, u32[]{:S(2)}) async-start(bf16[4,24,12820]{2,1,0:T(8,128)(2,1)} %bitcast.84), calls=%async_computation.2 | async-start | bytes 4964352 | tf_op jit(solution)/shard_map/all_to_all | solution.py:88
  642.1 6.0 copy-start.4
  642.1 10.4 %copy-start.6 = (s32[1280]{0:T(1024)S(1)}, s32[1280]{0:T(1024)}, u32[]{:S(2)}) copy-start(s32[1280]{0:T(1024)} %copy-done.5) | copy-start | bytes 15364
  642.1 10.4 %copy-start.8 = (s32[1280]{0:T(1024)S(1)}, s32[1280]{0:T(1024)}, u32[]{:S(2)}) copy-start(s32[1280]{0:T(1024)} %copy-done.7) | copy-start | bytes 15364
  642.1 10.4 %copy-start.10 = (pred[1280]{0:T(1024)(128)(4,1)S(1)}, pred[1280]{0:T(1024)(128)(4,1)}, u32[]{:S(2)}) copy-start(pred[1280]{0:T(1024)(128)(4,1)} %copy-done.9) | copy-start | bytes 3844
  642.1 10.4 %copy-start.12 = (pred[1280]{0:T(1024)(128)(4,1)S(1)}, pred[1280]{0:T(1024)(128)(4,1)}, u32[]{:S(2)}) copy-start(pred[1280]{0:T(1024)(128)(4,1)} %copy-done.11) | copy-start | bytes 3844
  642.2 178.7 %all-to-all-start.3 = ((bf16[2,24,640,2,80]{4,1,3,0,2:T(8,128)(2,1)}), bf16[2,24,640,2,80]{4,1,3,0,2:T(8,128)(2,1)}, u32[]{:S(2)}, u32[]{:S(2)}) async-start(bf16[2,24,640,2,80]{4,1,3,0,2:T(8,128)(2,1)} %copy.76), calls=%async_computation.3 | async-start | bytes 31457280 | tf_op jit(solution)/shard_map/all_to_all | solution.py:105
  942.3 18.3 %copy-start.1 = (bf16[96,96]{1,0:T(8,128)(2,1)S(1)}, bf16[96,96]{1,0:T(8,128)(2,1)}, u32[]{:S(2)}) copy-start(bf16[96,96]{1,0:T(8,128)(2,1)} %param.12) | copy-start | bytes 55300
where the time goes:
time: 973 us; the launch traced here: 961 us
  waiting for transfers between devices  416 us (43%)
  local copies, waits for them, and re-layouts  294 us (30%)
  other arithmetic  125 us (13%)
  matrix products  92.3 us (9%)
  starting transfers between devices  31.6 us (3%)
    all_to_all x1, waiting for transfers between devices, per_device(): lax.all_to_all(permuted, 'lat', split_axis=4, concat_axis=2, tiled=True)  173 us
    all_to_all x1, waiting for transfers between devices, per_device(): lax.all_to_all(synthesised, 'lat', split_axis=2, concat_axis=4, tiled=True)  138 us
    all_to_all x1, waiting for transfers between devices, per_device(): lax.all_to_all(padded, 'lev', split_axis=1, concat_axis=0, tiled=True)  52.9 us
    all_to_all x1, waiting for transfers between devices, per_device(): lax.all_to_all(solved_columns.astype(jnp.bfloat16), 'lev', split_axis=0,...  52.7 us
    reshape x2, local copies, waits for them, and re-layouts, per_device(): fourier_local.astype(jnp.bfloat16)  45.2 us
    all_to_all x1, local copies, waits for them, and re-layouts, per_device(): lax.all_to_all(synthesised, 'lat', split_axis=2, concat_axis=4, tiled=True)  33.7 us
    dot_general x1, other arithmetic, per_device(): jnp.dot(natural.reshape(-1, 2 * wave_count), inverse, preferred_element_t...  30 us
    dot_general x1, matrix products, per_device(): jnp.einsum('slj,fvlcsh->sfvchj', legendre, grouped, preferred_element_typ...  29.7 us
  transfers between devices with their start and end apart: 4, of which 4 were waited for; matrix products, arithmetic and copies ran while one was open for 4% of the time, Pallas kernels for 0%

commit v1 on v0

--- a/solution.py
+++ b/solution.py
@@ -3,6 +3,22 @@
 import jax.numpy as jnp
 from jax import lax
 from jax.sharding import PartitionSpec as P
+
+
+def pairwise_exchange(x, axis, split, join):
+    ways, here = (lax.axis_size(axis), lax.axis_index(axis))
+    width = x.shape[split] // ways
+    lengths = list(x.shape)
+    lengths[split] = width
+    height = lengths[join]
+    lengths[join] = height * ways
+    full = jnp.zeros(lengths, x.dtype)
+    for mask in range(ways):
+        part = lax.dynamic_slice_in_dim(x, (here ^ mask) * width, width, axis=split)
+        if mask:
+            part = lax.ppermute(part, axis, [(d, d ^ mask) for d in range(ways)])
+        full = lax.dynamic_update_slice_in_dim(full, part, (here ^ mask) * height, axis=join)
+    return full
 
 
 def tables(length, number):
@@ -56,7 +72,7 @@
     )
     column_order = jnp.stack([pair_order, wave_count - 1 - pair_order], axis=1).reshape(-1)
     permuted = jnp.take(fourier_local, column_order, axis=4)
-    received_bands = lax.all_to_all(permuted, "lat", split_axis=4, concat_axis=2, tiled=True)
+    received_bands = pairwise_exchange(permuted, "lat", 4, 2)
     grouped = received_bands.reshape(fields, levels, lat_count, 2, slot_count, 2)
     band_index = lax.axis_index("lat")
     local_waves = lax.dynamic_slice_in_dim(pair_order, band_index * slot_count, slot_count)

time: 973 us -> 1260 us (1.29)
  local copies, waits for them, and re-layouts: 294 us -> 723 us
  waiting for transfers between devices: 416 us -> 288 us
    dynamic_update_slice x0 -> x8, local copies, waits for them, and re-layouts: none -> 456 us  [pairwise_exchange(): lax.dynamic_update_slice_in_dim(full, part, (here ^ mask) * height, axis=...]
    all_to_all x1 -> x0, waiting for transfers between devices: 173 us -> none  [per_device(): lax.all_to_all(permuted, 'lat', split_axis=4, concat_axis=2, tiled=True)]
    ppermute x0 -> x7, waiting for transfers between devices: none -> 38.8 us  [pairwise_exchange(): part = lax.ppermute(part, axis, [(d, d ^ mask) for d in range(ways)])]
    all_to_all x1 -> x0, local copies, waits for them, and re-layouts: 27.2 us -> none  [per_device(): lax.all_to_all(permuted, 'lat', split_axis=4, concat_axis=2, tiled=True)]
    reshape x1 -> x0, local copies, waits for them, and re-layouts: 23.1 us -> none  [per_device(): received_bands.reshape(fields, levels, lat_count, 2, slot_count, 2)]
    ppermute x0 -> x7, local copies, waits for them, and re-layouts: none -> 13.2 us  [pairwise_exchange(): part = lax.ppermute(part, axis, [(d, d ^ mask) for d in range(ways)])]
  transfers between devices with their start and end apart: 4 -> 10, of which waited for: 4 -> 4; matrix products, arithmetic and copies ran while one was open for 4% -> 36% of each run, Pallas kernels for 0% -> 0%
where the time goes in v1:
time: 1260 us; the launch traced here: 1250 us
  local copies, waits for them, and re-layouts  723 us (57%)
  waiting for transfers between devices  288 us (23%)
  other arithmetic  120 us (10%)
  matrix products  92.3 us (7%)
  starting transfers between devices  25.3 us (2%)
    dynamic_update_slice x8, local copies, waits for them, and re-layouts, pairwise_exchange(): lax.dynamic_update_slice_in_dim(full, part, (here ^ mask) * height, axis=...  456 us
    all_to_all x1, waiting for transfers between devices, per_device(): lax.all_to_all(synthesised, 'lat', split_axis=2, concat_axis=4, tiled=True)  138 us
    all_to_all x1, waiting for transfers between devices, per_device(): lax.all_to_all(padded, 'lev', split_axis=1, concat_axis=0, tiled=True)  57.2 us
    all_to_all x1, waiting for transfers between devices, per_device(): lax.all_to_all(solved_columns.astype(jnp.bfloat16), 'lev', split_axis=0,...  53.6 us
    reshape x2, local copies, waits for them, and re-layouts, per_device(): fourier_local.astype(jnp.bfloat16)  45.2 us
    ppermute x7, waiting for transfers between devices, pairwise_exchange(): part = lax.ppermute(part, axis, [(d, d ^ mask) for d in range(ways)])  38.8 us
    all_to_all x1, local copies, waits for them, and re-layouts, per_device(): lax.all_to_all(synthesised, 'lat', split_axis=2, concat_axis=4, tiled=True)  33.7 us
    dot_general x1, other arithmetic, per_device(): jnp.dot(natural.reshape(-1, 2 * wave_count), inverse, preferred_element_t...  30 us
  transfers between devices with their start and end apart: 10, of which 4 were waited for; matrix products, arithmetic and copies ran while one was open for 36% of the time, Pallas kernels for 0%

profile of v1, /device:TPU:0, one launch (start us, length us, event | category | flops | bytes accessed | tf_op | source)
XLA Modules:
  0.0 1249.8 jit_solution(11737598205173073039)
XLA Ops:
  25.3 27.6 %multiply_convert_fusion.4 = bf16[1280,1280]{1,0:T(8,128)(2,1)S(1)} fusion(s32[1280]{0:T(1024)S(1)} %get-tuple-element.22, s32[1280]{0:T(1024)S(1)} %get-tuple-element.23, pred[1280]{0:T(1024)(128)(4,1)S(1)} %get-tuple-element.25, pred[1280]{0:T(1024)(128)(4,1)S(1)} %get-tuple-element.24), kind=kLoop, calls=%fused_computation.46.clone.clone.1 | loop fusion | flops 22937600 | bytes 3289600 | tf_op jit(solution)/shard_map/dot_general | solution.py:67
  71.8 19.3 %reshape.232 = bf16[2,24,80,2,640]{4,3,2,1,0:T(2,128)(2,1)} reshape(bf16[3840,1280]{1,0:T(8,128)(2,1)} %convolution_convert_fusion.1) | data formatting | bytes 19660800 | tf_op jit(solution)/shard_map/reshape | solution.py:70
  91.1 25.9 %copy.85 = bf16[2,24,80,2,640]{2,1,3,0,4:T(8,128)(2,1)} copy(bf16[2,24,80,2,640]{4,3,2,1,0:T(2,128)(2,1)} %reshape.232) | data formatting | bytes 19660800 | tf_op jit(solution)/shard_map/reshape | solution.py:70
  117.1 25.1 %gather_fusion = bf16[640,2,24,80,2]{3,2,4,1,0:T(8,128)(2,1)} fusion(bf16[2,24,80,2,640]{2,1,3,0,4:T(8,128)(2,1)} %copy.85, s32[1024]{0:T(1024)S(1)} %pad_clamp_fusion.1), kind=kCustom, calls=%fused_computation.clone | custom fusion | bytes 19663360 | tf_op jit(solution)/shard_map/jit(_take)/gather | solution.py:74
  163.5 38.7 %collective-permute-done.1 = bf16[2,24,80,2,80]{2,1,3,0,4:T(8,128)(2,1)S(1)} collective-permute-done((bf16[2,24,80,2,80]{2,1,3,0,4:T(8,128)(2,1)S(1)}, bf16[2,24,80,2,80]{2,1,3,0,4:T(8,128)(2,1)S(1)}, u32[]{:S(2)}, u32[]{:S(2)}) %collective-permute-start.1) | collective-permute-done | bytes 1228832 | tf_op jit(solution)/shard_map/ppermute | solution.py:19
  209.1 23.1 %dynamic_update_slice.24 = bf16[2,24,640,2,80]{2,1,4,3,0:T(8,128)(2,1)} dynamic-update-slice(bf16[2,24,640,2,80]{2,1,4,3,0:T(8,128)(2,1)} %broadcast_in_dim.63, bf16[2,24,80,2,80]{2,1,4,3,0:T(8,128)(2,1)S(1)} %copy.86, s32[]{:T(128)} %constant.30.clone.1, s32[]{:T(128)} %constant.30.clone.1, s32[]{:T(128)S(6)} %select_n.127, s32[]{:T(128)} %constant.30.clone.1, s32[]{:T(128)} %constant.30.clone.1) | dynamic-update-slice | bytes 2457604 | tf_op jit(solution)/shard_map/dynamic_update_slice | solution.py:20
  235.0 61.9 %dynamic_update_slice.25 = bf16[2,24,640,2,80]{2,1,4,3,0:T(8,128)(2,1)} dynamic-update-slice(bf16[2,24,640,2,80]{2,1,4,3,0:T(8,128)(2,1)} %dynamic_update_slice.24, bf16[2,24,80,2,80]{2,1,4,3,0:T(8,128)(2,1)S(1)} %copy.87, s32[]{:T(128)} %constant.30.clone.1, s32[]{:T(128)} %constant.30.clone.1, s32[]{:T(128)S(6)} %select_n.128, s32[]{:T(128)} %constant.30.clone.1, s32[]{:T(128)} %constant.30.clone.1) | dynamic-update-slice | bytes 2457604 | tf_op jit(solution)/shard_map/dynamic_update_slice | solution.py:20
  298.8 61.9 %dynamic_update_slice.26 = bf16[2,24,640,2,80]{2,1,4,3,0:T(8,128)(2,1)} dynamic-update-slice(bf16[2,24,640,2,80]{2,1,4,3,0:T(8,128)(2,1)} %dynamic_update_slice.25, bf16[2,24,80,2,80]{2,1,4,3,0:T(8,128)(2,1)S(1)} %copy.88, s32[]{:T(128)} %constant.30.clone.1, s32[]{:T(128)} %constant.30.clone.1, s32[]{:T(128)S(6)} %select_n.129, s32[]{:T(128)} %constant.30.clone.1, s32[]{:T(128)} %constant.30.clone.1) | dynamic-update-slice | bytes 2457604 | tf_op jit(solution)/shard_map/dynamic_update_slice | solution.py:20
  362.5 62.3 %dynamic_update_slice.27 = bf16[2,24,640,2,80]{2,1,4,3,0:T(8,128)(2,1)} dynamic-update-slice(bf16[2,24,640,2,80]{2,1,4,3,0:T(8,128)(2,1)} %dynamic_update_slice.26, bf16[2,24,80,2,80]{2,1,4,3,0:T(8,128)(2,1)S(1)} %copy.89, s32[]{:T(128)} %constant.30.clone.1, s32[]{:T(128)} %constant.30.clone.1, s32[]{:T(128)S(6)} %select_n.130, s32[]{:T(128)} %constant.30.clone.1, s32[]{:T(128)} %constant.30.clone.1) | dynamic-update-slice | bytes 2457604 | tf_op jit(solution)/shard_map/dynamic_update_slice | solution.py:20
  426.7 61.9 %dynamic_update_slice.28 = bf16[2,24,640,2,80]{2,1,4,3,0:T(8,128)(2,1)} dynamic-update-slice(bf16[2,24,640,2,80]{2,1,4,3,0:T(8,128)(2,1)} %dynamic_update_slice.27, bf16[2,24,80,2,80]{2,1,4,3,0:T(8,128)(2,1)S(1)} %copy.90, s32[]{:T(128)} %constant.30.clone.1, s32[]{:T(128)} %constant.30.clone.1, s32[]{:T(128)S(6)} %select_n.131, s32[]{:T(128)} %constant.30.clone.1, s32[]{:T(128)} %constant.30.clone.1) | dynamic-update-slice | bytes 2457604 | tf_op jit(solution)/shard_map/dynamic_update_slice | solution.py:20
  490.5 61.9 %dynamic_update_slice.29 = bf16[2,24,640,2,80]{2,1,4,3,0:T(8,128)(2,1)} dynamic-update-slice(bf16[2,24,640,2,80]{2,1,4,3,0:T(8,128)(2,1)} %dynamic_update_slice.28, bf16[2,24,80,2,80]{2,1,4,3,0:T(8,128)(2,1)S(1)} %copy.91, s32[]{:T(128)} %constant.30.clone.1, s32[]{:T(128)} %constant.30.clone.1, s32[]{:T(128)S(6)} %select_n.132, s32[]{:T(128)} %constant.30.clone.1, s32[]{:T(128)} %constant.30.clone.1) | dynamic-update-slice | bytes 2457604 | tf_op jit(solution)/shard_map/dynamic_update_slice | solution.py:20
  554.3 61.9 %dynamic_update_slice.30 = bf16[2,24,640,2,80]{2,1,4,3,0:T(8,128)(2,1)} dynamic-update-slice(bf16[2,24,640,2,80]{2,1,4,3,0:T(8,128)(2,1)} %dynamic_update_slice.29, bf16[2,24,80,2,80]{2,1,4,3,0:T(8,128)(2,1)S(1)} %copy.92, s32[]{:T(128)} %constant.30.clone.1, s32[]{:T(128)} %constant.30.clone.1, s32[]{:T(128)S(6)} %select_n.133, s32[]{:T(128)} %constant.30.clone.1, s32[]{:T(128)} %constant.30.clone.1) | dynamic-update-slice | bytes 2457604 | tf_op jit(solution)/shard_map/dynamic_update_slice | solution.py:20
  618.1 61.3 %dynamic_update_slice.31 = bf16[2,24,640,2,80]{2,1,4,3,0:T(8,128)(2,1)} dynamic-update-slice(bf16[2,24,640,2,80]{2,1,4,3,0:T(8,128)(2,1)} %dynamic_update_slice.30, bf16[2,24,80,2,80]{2,1,4,3,0:T(8,128)(2,1)S(1)} %copy.93, s32[]{:T(128)} %constant.30.clone.1, s32[]{:T(128)} %constant.30.clone.1, s32[]{:T(128)S(6)} %select_n.134, s32[]{:T(128)} %constant.30.clone.1, s32[]{:T(128)} %constant.30.clone.1) | dynamic-update-slice | bytes 2457604 | tf_op jit(solution)/shard_map/dynamic_update_slice | solution.py:20
  679.4 29.7 %fusion.2 = f32[40,2,24,2,2,641]{5,2,4,3,1,0:T(8,128)} fusion(bf16[40,640,641,1,1,1]{1,0,2,5,4,3:T(8,128)(2,1)} %bitcast.72, bf16[2,24,640,2,40,2]{2,1,5,4,3,0:T(8,128)(2,1)} %bitcast.71), kind=kOutput, calls=%fused_computation.5 | convolution fusion | flops 6301286400 | bytes 62341120 | tf_op jit(solution)/shard_map/slj,fvlcsh->sfvchj/dot_general | solution.py:80
  738.1 57.2 %all-to-all-done = bf16[24,4,12820]{2,0,1:T(8,128)(2,1)S(1)} async-done(((bf16[24,4,12820]{2,0,1:T(8,128)(2,1)}), bf16[24,4,12820]{2,0,1:T(8,128)(2,1)S(1)}, u32[]{:S(2)}, u32[]{:S(2)}) %all-to-all-start) | async-done | bytes 2461472 | tf_op jit(solution)/shard_map/all_to_all | solution.py:94
  806.4 53.6 %all-to-all-done.1 = bf16[4,24,12820]{2,1,0:T(8,128)(2,1)} async-done(((bf16[4,24,12820]{2,1,0:T(8,128)(2,1)}), bf16[4,24,12820]{2,1,0:T(8,128)(2,1)}, u32[]{:S(2)}, u32[]{:S(2)}) %all-to-all-start.1) | async-done | bytes 2461472 | tf_op jit(solution)/shard_map/all_to_all | solution.py:104
  880.0 22.3 %convert_bitcast_fusion = bf16[2,24,640,2,40,2]{2,1,5,3,0,4:T(8,128)(2,1)} fusion(bf16[40,640,641,1,1,1]{1,0,2,5,4,3:T(8,128)(2,1)} %bitcast.73, bf16[40,2,24,2,1,641]{5,2,3,0,4,1:T(8,128)(2,1)S(1)} %get-tuple-element.19, bf16[40,2,24,2,1,641]{5,2,3,0,4,1:T(8,128)(2,1)S(1)} %get-tuple-element.18), kind=kOutput, calls=%fused_computation.30 | convolution fusion | flops 6311124480 | bytes 52495360 | tf_op jit(solution)/shard_map/slj,sfvchj->fvlcsh/dot_general | solution.py:115
  910.7 20.1 %copy.104 = bf16[2,24,640,2,80]{4,1,3,0,2:T(8,128)(2,1)} copy(bf16[2,24,640,2,80]{2,1,4,3,0:T(8,128)(2,1)} %bitcast.70) | data formatting | bytes 19660800 | tf_op jit(solution)/shard_map/reshape | solution.py:118
  941.2 30.0 %fusion.83 = bf16[1280,1280,1,1]{1,0,3,2:T(8,128)(2,1)S(1)} fusion(s32[1280]{0:T(1024)S(1)} %copy-done.8, s32[1280]{0:T(1024)S(1)} %copy-done.10, pred[1280]{0:T(1024)(128)(4,1)S(1)} %copy-done.14, pred[1280]{0:T(1024)(128)(4,1)S(1)} %copy-done.12), kind=kLoop, calls=%fused_computation.58.clone.clone.1 | loop fusion | flops 27852800 | bytes 3289600 | tf_op jit(solution)/shard_map/dot_general | solution.py:128
  971.2 138.4 %all-to-all-done.2 = bf16[2,24,640,2,80]{4,1,3,0,2:T(8,128)(2,1)} async-done(((bf16[2,24,640,2,80]{4,1,3,0,2:T(8,128)(2,1)}), bf16[2,24,640,2,80]{4,1,3,0,2:T(8,128)(2,1)}, u32[]{:S(2)}, u32[]{:S(2)}) %all-to-all-start.2) | async-done | bytes 9830432 | tf_op jit(solution)/shard_map/all_to_all | solution.py:121
  1109.5 33.7 %copy.115 = bf16[2,24,80,2,8,80]{2,1,3,0,5,4:T(8,128)(2,1)} copy(bf16[2,24,80,2,8,80]{5,1,3,0,2,4:T(8,128)(2,1)} %bitcast.30) | data formatting | bytes 19660800 | tf_op jit(solution)/shard_map/all_to_all | solution.py:121
  1143.3 25.0 %gather_fusion.1 = bf16[640,2,24,80,2]{3,2,4,1,0:T(8,128)(2,1)} fusion(bf16[2,24,80,2,640]{2,1,3,0,4:T(8,128)(2,1)} %bitcast.69, s32[1024]{0:T(1024)S(1)} %pad_clamp_fusion), kind=kCustom, calls=%fused_computation.1.clone | custom fusion | bytes 19663360 | tf_op jit(solution)/shard_map/jit(_take)/gather | solution.py:127
  1182.2 27.0 %copy.107 = bf16[2,24,80,2,640]{4,3,2,1,0:T(2,128)(2,1)} copy(bf16[2,24,80,2,640]{2,1,3,0,4:T(8,128)(2,1)} %select_bitcast_fusion) | data formatting | bytes 19660800 | tf_op jit(solution)/shard_map/jit(_take)/select_n | solution.py:127
  1209.2 21.8 %dot_general.28 = bf16[2,24,80,1280]{3,2,1,0:T(8,128)(2,1)} reshape(bf16[2,24,80,2,640]{4,3,2,1,0:T(2,128)(2,1)} %copy.107) | data formatting | bytes 19660800 | tf_op jit(solution)/shard_map/dot_general | solution.py:128
  (101 shorter events, 197.3 us)
Async XLA Ops:
  0.0 795.3 %copy-start = (bf16[96,96]{1,0:T(8,128)(2,1)S(1)}, bf16[96,96]{1,0:T(8,128)(2,1)}, u32[]{:S(2)}) copy-start(bf16[96,96]{1,0:T(8,128)(2,1)} %param.12) | copy-start | bytes 55300
  0.0 25.3 %copy-start.7 = (s32[1280]{0:T(1024)}, s32[1280]{0:T(1024)S(1)}, u32[]{:S(2)}) copy-start(s32[1280]{0:T(1024)S(1)} %get-tuple-element.22) | copy-start | bytes 15364
  0.0 25.3 %copy-start.9 = (s32[1280]{0:T(1024)}, s32[1280]{0:T(1024)S(1)}, u32[]{:S(2)}) copy-start(s32[1280]{0:T(1024)S(1)} %get-tuple-element.23) | copy-start | bytes 15364
  0.0 25.2 %copy-start.11 = (pred[1280]{0:T(1024)(128)(4,1)}, pred[1280]{0:T(1024)(128)(4,1)S(1)}, u32[]{:S(2)}) copy-start(pred[1280]{0:T(1024)(128)(4,1)S(1)} %get-tuple-element.24) | copy-start | bytes 3844
  0.1 25.2 %copy-start.13 = (pred[1280]{0:T(1024)(128)(4,1)}, pred[1280]{0:T(1024)(128)(4,1)S(1)}, u32[]{:S(2)}) copy-start(pred[1280]{0:T(1024)(128)(4,1)S(1)} %get-tuple-element.25) | copy-start | bytes 3844
  1.6 15.0 %copy-start.5 = (s32[320,2]{1,0:T(8,128)}, s32[320,2]{1,0:T(8,128)S(1)}, u32[]{:S(2)}) copy-start(s32[320,2]{1,0:T(8,128)S(1)} %copy.83) | copy-start | bytes 7684
  155.6 4.9 collective-permute-start
  156.1 46.2 %collective-permute-start.1 = (bf16[2,24,80,2,80]{2,1,3,0,4:T(8,128)(2,1)S(1)}, bf16[2,24,80,2,80]{2,1,3,0,4:T(8,128)(2,1)S(1)}, u32[]{:S(2)}, u32[]{:S(2)}) collective-permute-start(bf16[2,24,80,2,80]{2,1,3,0,4:T(8,128)(2,1)S(1)} %get-tuple-element.15), channel_id=1, source_target_pairs={{0,8},{4,12},{8,0},{12,4},{16,24},{20,28},{24,16},{28,20},{1,9},{5... | collective-permute-start | bytes 3686408 | tf_op jit(solution)/shard_map/ppermute | solution.py:19
  158.6 202.1 %collective-permute-start.2 = (bf16[2,24,80,2,80]{2,1,3,0,4:T(8,128)(2,1)}, bf16[2,24,80,2,80]{2,1,3,0,4:T(8,128)(2,1)}, u32[]{:S(2)}, u32[]{:S(2)}) collective-permute-start(bf16[2,24,80,2,80]{2,1,3,0,4:T(8,128)(2,1)} %get-tuple-element.14), channel_id=1, source_target_pairs={{0,12},{4,8},{8,4},{12,0},{16,28},{20,24},{24,20},{28,16},{1,13},{... | collective-permute-start | bytes 3686408 | tf_op jit(solution)/shard_map/ppermute | solution.py:19
  158.7 266.1 %collective-permute-start.3 = (bf16[2,24,80,2,80]{2,1,3,0,4:T(8,128)(2,1)}, bf16[2,24,80,2,80]{2,1,3,0,4:T(8,128)(2,1)}, u32[]{:S(2)}, u32[]{:S(2)}) collective-permute-start(bf16[2,24,80,2,80]{2,1,3,0,4:T(8,128)(2,1)} %get-tuple-element.13), channel_id=1, source_target_pairs={{0,16},{4,20},{8,24},{12,28},{16,0},{20,4},{24,8},{28,12},{1,17},{... | collective-permute-start | bytes 3686408 | tf_op jit(solution)/shard_map/ppermute | solution.py:19
  160.5 328.1 %collective-permute-start.4 = (bf16[2,24,80,2,80]{2,1,3,0,4:T(8,128)(2,1)}, bf16[2,24,80,2,80]{2,1,3,0,4:T(8,128)(2,1)}, u32[]{:S(2)}, u32[]{:S(2)}) collective-permute-start(bf16[2,24,80,2,80]{2,1,3,0,4:T(8,128)(2,1)} %get-tuple-element.12), channel_id=1, source_target_pairs={{0,20},{4,16},{8,28},{12,24},{16,4},{20,0},{24,12},{28,8},{1,21},{... | collective-permute-start | bytes 3686408 | tf_op jit(solution)/shard_map/ppermute | solution.py:19
  160.5 43.7 %copy-start.4 = (bf16[2,24,80,2,80]{2,1,3,0,4:T(8,128)(2,1)}, bf16[2,24,80,2,80]{2,1,3,0,4:T(8,128)(2,1)S(1)}, u32[]{:S(2)}) copy-start(bf16[2,24,80,2,80]{2,1,3,0,4:T(8,128)(2,1)S(1)} %collective-permute-done) | copy-start | bytes 3686404
  160.5 391.9 %collective-permute-start.5 = (bf16[2,24,80,2,80]{2,1,3,0,4:T(8,128)(2,1)}, bf16[2,24,80,2,80]{2,1,3,0,4:T(8,128)(2,1)}, u32[]{:S(2)}, u32[]{:S(2)}) collective-permute-start(bf16[2,24,80,2,80]{2,1,3,0,4:T(8,128)(2,1)} %get-tuple-element.11), channel_id=1, source_target_pairs={{0,24},{4,28},{8,16},{12,20},{16,8},{20,12},{24,0},{28,4},{1,25},{... | collective-permute-start | bytes 3686408 | tf_op jit(solution)/shard_map/ppermute | solution.py:19
  202.3 413.9 %collective-permute-start.6 = (bf16[2,24,80,2,80]{2,1,3,0,4:T(8,128)(2,1)}, bf16[2,24,80,2,80]{2,1,3,0,4:T(8,128)(2,1)}, u32[]{:S(2)}, u32[]{:S(2)}) collective-permute-start(bf16[2,24,80,2,80]{2,1,3,0,4:T(8,128)(2,1)} %get-tuple-element.10), channel_id=1, source_target_pairs={{0,28},{4,24},{8,20},{12,16},{16,12},{20,8},{24,4},{28,0},{1,29},{... | collective-permute-start | bytes 3686408 | tf_op jit(solution)/shard_map/ppermute | solution.py:19
  729.1 66.1 %copy-start.15 = (f32[96]{0:T(128)S(1)}, f32[96]{0:T(128)}, u32[]{:S(2)}) copy-start(f32[96]{0:T(128)} %param.13) | copy-start | bytes 1156
  732.6 62.7 %all-to-all-start = ((bf16[24,4,12820]{2,0,1:T(8,128)(2,1)}), bf16[24,4,12820]{2,0,1:T(8,128)(2,1)S(1)}, u32[]{:S(2)}, u32[]{:S(2)}) async-start(bf16[24,4,12820]{2,0,1:T(8,128)(2,1)} %copy.98), calls=%async_computation | async-start | bytes 4964352 | tf_op jit(solution)/shard_map/all_to_all | solution.py:94
  798.3 61.7 %all-to-all-start.1 = ((bf16[4,24,12820]{2,1,0:T(8,128)(2,1)}), bf16[4,24,12820]{2,1,0:T(8,128)(2,1)}, u32[]{:S(2)}, u32[]{:S(2)}) async-start(bf16[4,24,12820]{2,1,0:T(8,128)(2,1)} %bitcast.77), calls=%async_computation.1 | async-start | bytes 4964352 | tf_op jit(solution)/shard_map/all_to_all | solution.py:104
  930.8 6.0 copy-start.6
  930.8 10.4 copy-start.8
  930.8 10.4 copy-start.10
  930.8 10.4 copy-start.12
  930.8 10.4 copy-start.14
  930.8 178.7 %all-to-all-start.2 = ((bf16[2,24,640,2,80]{4,1,3,0,2:T(8,128)(2,1)}), bf16[2,24,640,2,80]{4,1,3,0,2:T(8,128)(2,1)}, u32[]{:S(2)}, u32[]{:S(2)}) async-start(bf16[2,24,640,2,80]{4,1,3,0,2:T(8,128)(2,1)} %copy.104), calls=%async_computation.2 | async-start | bytes 31457280 | tf_op jit(solution)/shard_map/all_to_all | solution.py:121
  1231.0 18.3 %copy-start.1 = (bf16[96,96]{1,0:T(8,128)(2,1)S(1)}, bf16[96,96]{1,0:T(8,128)(2,1)}, u32[]{:S(2)}) copy-start(bf16[96,96]{1,0:T(8,128)(2,1)} %param.12) | copy-start | bytes 55300
  (2 other events, 6.4 us)
